TPU v7x, 32 devices: a whole 2x2x4 slice. The times are simulated.
32 devices in a mesh: seq: 16 (over z, x, core), fsdp: 2 (over y).
Axes of the slice: x: 2, y: 2, z: 4, core: 2. Of those that a mesh axis runs over, the one named last changes fastest.
Arguments:
- hidden: bfloat16 [2, 4096, 1024], P('fsdp', 'seq')
- w_qkv: bfloat16 [1024, 3072], P('fsdp')
- cond_vec: bfloat16 [1024], replicated, may hold values from -6 to 6
- head_w: bfloat16 [1024], replicated, may hold values from -0.1875 to 0.1875
- blocks: int32 [2, 64, 5], P('fsdp', 'seq'), may hold values from 0 to 63, as said below
- counts: int32 [2, 64], P('fsdp', 'seq'), may hold values from 1 to 4, 128 in all within a row
- time_idx: int32 [2, 4096], P('fsdp', 'seq'), may hold values from 0 to 999
- cond_mask: int32 [2, 4096], P('fsdp', 'seq'), may hold values 0 or 1
- noise: float32 [2, 4096], P('fsdp', 'seq'), may hold values from -6 to 6
Outputs:
- d_hidden: bfloat16 [2, 4096, 1024], P('fsdp', 'seq')
- grad_qkv: float32 [1024, 3072], P('fsdp')
Inputs may be any that keep to these rules, and one draw needn't show every extreme that they name: Each list holds 5 distinct blocks of its own sequence: slot 0 is the query block itself, slot 1 a block exactly 4 blocks before or after it around the cycle of 64 blocks, and the other slots blocks within 4 of it around that cycle. Each sequence's counts sum to 128.
All inputs are finite; a program needn't handle non-finite values. No bound on the sum of `counts` or of `cond_mask` on one device may be relied on, other than what follows from the above.
Results may differ from a plain program's by a relative error of at most 0.014.
Values may be sent and summed in bfloat16 or wider, within the bound.
A program may use at most 128 MiB of HBM per device.

v0:
```python
import math
import jax
import jax.numpy as jnp
from jax import lax
from jax.sharding import PartitionSpec as P

HD = 64
BLK = 64
REACH = 4
NB = 5
EPS = 1e-05


def extended_2(cells, sides, width):
    for axis, dim in sides:
        count = lax.axis_size(axis)
        head = lax.slice_in_dim(cells, 0, width, axis=dim)
        tail = lax.slice_in_dim(cells, cells.shape[dim] - width, cells.shape[dim], axis=dim)
        cells = jnp.concatenate(
            [
                lax.ppermute(tail, axis, [(i, (i + 1) % count) for i in range(count)]),
                cells,
                lax.ppermute(head, axis, [((i + 1) % count, i) for i in range(count)]),
            ],
            axis=dim,
        )
    return cells


def passed_along(value, axis, steps):
    count = lax.axis_size(axis)
    pairs = [(source, (source + steps) % count) for source in range(count)]
    return lax.ppermute(value, axis, pairs)


def time_features(steps_idx, width):
    half = width // 2
    freq = jnp.exp(-math.log(10000.0) * jnp.arange(half, dtype=jnp.float32) / half)
    angle = steps_idx.astype(jnp.float32)[:, None] * freq[None, :]
    return jnp.concatenate([jnp.sin(angle), jnp.cos(angle)], axis=1)


def body(hidden, w_qkv, cond_vec, head_w, blocks, counts, time_idx, cond_mask, noise):
    tokens = hidden.shape[1]
    width = hidden.shape[2]
    heads = width // HD
    scale = HD ** (-0.5)
    local_blocks = tokens // BLK
    ext_blocks = local_blocks + 2 * REACH
    group_heads = 4
    head_groups = heads // group_heads
    cond = cond_mask[0].astype(jnp.float32)
    head_row = head_w.astype(jnp.float32)
    h_in = (
        hidden[0].astype(jnp.float32)
        + cond[:, None] * cond_vec.astype(jnp.float32)[None, :]
        + time_features(time_idx[0], width)
    )
    inv = lax.rsqrt(jnp.mean(h_in * h_in, axis=1, keepdims=True) + EPS)
    normed = (h_in * inv).astype(jnp.bfloat16)
    columns = normed
    qkv = jnp.dot(
        columns,
        lax.all_gather(w_qkv, "fsdp", axis=0, tiled=True),
        preferred_element_type=jnp.float32,
    ).astype(jnp.bfloat16)
    query = (
        qkv[:, :width]
        .reshape(local_blocks, BLK, head_groups, group_heads, HD)
        .transpose(2, 0, 1, 3, 4)
    )
    extended = extended_2(qkv[:, width:], (("seq", 0),), REACH * BLK)
    extended = extended.reshape(ext_blocks, BLK, 2 * width)
    blocks_all = local_blocks * lax.axis_size("seq")
    first_block = lax.axis_index("seq") * local_blocks
    ext_index = jnp.remainder(blocks[0] - first_block + REACH, blocks_all)
    chosen = extended[ext_index].reshape(local_blocks, NB * BLK, 2, head_groups, group_heads, HD)
    chosen = chosen.transpose(3, 0, 1, 2, 4, 5)
    valid = lax.broadcasted_iota(jnp.int32, (local_blocks, NB), 1) <= counts[0][:, None]
    key_valid = jnp.repeat(valid, BLK, axis=1)

    def softmax_probs(group_query, keys):
        scores = (
            jnp.einsum("tqhd,tkhd->thqk", group_query, keys, preferred_element_type=jnp.float32)
            * scale
        )
        scores = jnp.where(key_valid[:, None, None, :], scores, -1e30)
        top = jnp.max(scores, axis=3, keepdims=True)
        expo = jnp.exp(scores - top)
        return expo / jnp.sum(expo, axis=3, keepdims=True)

    def forward_group(items):
        group_query, group_pairs = items
        probs = softmax_probs(group_query, group_pairs[:, :, 0])
        probs_b = probs.astype(jnp.bfloat16)
        return jnp.einsum(
            "thqk,tkhd->tqhd", probs_b, group_pairs[:, :, 1], preferred_element_type=jnp.float32
        ).astype(jnp.bfloat16)

    attn_groups = lax.map(forward_group, (query, chosen))
    attn = attn_groups.transpose(1, 2, 0, 3, 4).reshape(tokens, width)
    h_out = h_in + attn.astype(jnp.float32)
    net = jnp.sum(h_out * head_row[None, :], axis=1)
    d_net = 2.0 * (1.0 - cond) * (net + noise[0])
    d_out = d_net[:, None] * head_row[None, :]
    d_attn = (
        d_out.astype(jnp.bfloat16)
        .reshape(local_blocks, BLK, head_groups, group_heads, HD)
        .transpose(2, 0, 1, 3, 4)
    )

    def backward_group(items):
        group_query, group_pairs, group_d_attn, group_attn = items
        keys = group_pairs[:, :, 0]
        vals = group_pairs[:, :, 1]
        probs = softmax_probs(group_query, keys)
        probs_b = probs.astype(jnp.bfloat16)
        delta = jnp.sum(group_d_attn.astype(jnp.float32) * group_attn.astype(jnp.float32), axis=3)
        d_probs = jnp.einsum(
            "tqhd,tkhd->thqk", group_d_attn, vals, preferred_element_type=jnp.float32
        )
        d_scores = (probs * (d_probs - jnp.transpose(delta, (0, 2, 1))[..., None])).astype(
            jnp.bfloat16
        )
        d_query = (
            jnp.einsum("thqk,tkhd->tqhd", d_scores, keys, preferred_element_type=jnp.float32)
            * scale
        )
        d_keys = (
            jnp.einsum("thqk,tqhd->tkhd", d_scores, group_query, preferred_element_type=jnp.float32)
            * scale
        )
        d_vals = jnp.einsum(
            "thqk,tqhd->tkhd", probs_b, group_d_attn, preferred_element_type=jnp.float32
        )
        return (d_query, jnp.stack([d_keys, d_vals], axis=2))

    d_query_groups, d_pair_groups = lax.map(backward_group, (query, chosen, d_attn, attn_groups))
    d_query = d_query_groups.transpose(1, 2, 0, 3, 4).reshape(tokens, width)
    d_chosen = d_pair_groups.transpose(1, 2, 3, 0, 4, 5).reshape(local_blocks * NB, BLK, 2 * width)
    d_extended = (
        jnp.zeros((ext_blocks, BLK, 2 * width), jnp.float32).at[ext_index.reshape(-1)].add(d_chosen)
    )
    from_right = passed_along(d_extended[:REACH].astype(jnp.bfloat16), "seq", -1).astype(
        jnp.float32
    )
    from_left = passed_along(
        d_extended[ext_blocks - REACH :].astype(jnp.bfloat16), "seq", 1
    ).astype(jnp.float32)
    d_pairs = d_extended[REACH : REACH + local_blocks]
    d_pairs = d_pairs.at[:REACH].add(from_left)
    d_pairs = d_pairs.at[local_blocks - REACH :].add(from_right)
    d_qkv = jnp.concatenate([d_query, d_pairs.reshape(tokens, 2 * width)], axis=1).astype(
        jnp.bfloat16
    )
    columns = normed
    partial_grad = lax.psum_scatter(
        jnp.einsum("tc,tk->ck", columns, d_qkv, preferred_element_type=jnp.float32).astype(
            jnp.bfloat16
        ),
        "fsdp",
        scatter_dimension=0,
        tiled=True,
    )
    grad = lax.psum(partial_grad, "seq").astype(jnp.float32)
    d_normed = lax.dot_general(
        d_qkv,
        lax.all_gather(w_qkv, "fsdp", axis=0, tiled=True),
        (((1,), (1,)), ((), ())),
        preferred_element_type=jnp.float32,
    )
    d_in = inv * (d_normed - h_in * inv * inv * jnp.mean(d_normed * h_in, axis=1, keepdims=True))
    d_hidden = (d_out + d_in).astype(jnp.bfloat16)
    return (d_hidden[None], grad)


def solution(mesh):
    return jax.shard_map(
        body,
        mesh=mesh,
        in_specs=(
            P("fsdp", "seq", None),
            P("fsdp", None),
            P(),
            P(),
            P("fsdp", "seq", None),
            P("fsdp", "seq"),
            P("fsdp", "seq"),
            P("fsdp", "seq"),
            P("fsdp", "seq"),
        ),
        out_specs=(P("fsdp", "seq", None), P("fsdp", None)),
        check_vma=False,
    )
```

profile of v0, /device:TPU:0, one launch (start us, length us, event | category | flops | bytes accessed | tf_op | source)
XLA Modules:
  0.0 576.1 jit_solution(7214676377013264921)
XLA Ops:
  10.4 82.3 %all-gather.2.cloned.1.call-done = bf16[1024,3072]{1,0:T(8,128)(2,1)} async-done(((bf16[512,3072]{1,0:T(8,128)(2,1)}), bf16[1024,3072]{1,0:T(8,128)(2,1)}) %all-gather.2.cloned.1.call-update) | async-done | bytes 6291472 | tf_op jit(solution)/shard_map/all_gather | solution.py:64
  92.7 4.6 convolution_convert_fusion.2
  98.5 4.4 collective-permute-start.1
  107.7 7.9 %collective-permute-done = bf16[256,2048]{1,0:T(8,128)(2,1)} collective-permute-done((bf16[256,2048]{1,0:T(8,128)(2,1)S(1)}, bf16[256,2048]{1,0:T(8,128)(2,1)}, u32[]{:S(2)}, u32[]{:S(2)}) %collective-permute-start) | collective-permute-done | bytes 1048608 | tf_op jit(solution)/shard_map/ppermute | solution.py:21
  117.6 4.1 gather_fusion
  121.8 18.6 %reshape.286 = bf16[4,320,2,4,4,64]{5,4,3,2,1,0:T(4,128)(2,1)} reshape(bf16[20,64,2048]{2,1,0:T(8,128)(2,1)} %gather_fusion) | data formatting | bytes 10485760 | tf_op jit(solution)/shard_map/reshape | solution.py:77
  140.4 17.9 %copy.19 = bf16[4,4,320,2,4,64]{2,5,4,1,3,0:T(8,128)(2,1)} copy(bf16[4,4,320,2,4,64]{5,4,0,3,2,1:T(4,128)(2,1)} %bitcast.173) | data formatting | bytes 10485760
  158.3 26.0 %while.28 = (s32[]{:T(128)}, bf16[4,4,64,4,64]{2,4,3,1,0:T(8,128)(2,1)S(1)}, bf16[4,4,320,2,4,64]{2,5,4,1,3,0:T(8,128)(2,1)}, bf16[4,4,64,4,64]{4,2,3,1,0:T(8,128)(2,1)}, pred[4,5]{1,0:T(4,128)(4,1)S(1)}, /*index=5*/s32[]{:T(128)}) while((s32[]{:T(128)}, bf16[4,4,64,4,64]{2,4,3,1,0:T(8,128)(2,1)S(1)}, ...), condition=%wide.region_4.5_spmd.clone, body=%wide.region_1.4_spmd.clone.sunk | while | flops 128845440 | bytes 5787997 | solution.py:100
  161.7 3.0 fusion.100
  168.3 3.0 fusion.100
  174.8 3.0 fusion.100
  181.3 3.0 fusion.100
  186.9 2.5 copy.20
  194.7 67.3 %while.29 = (s32[]{:T(128)}, bf16[4,4,64,4,64]{2,4,3,1,0:T(8,128)(2,1)}, f32[4,4,320,2,4,64]{2,5,4,1,3,0:T(8,128)}, bf16[4,4,320,2,4,64]{2,5,4,1,3,0:T(8,128)(2,...) while((s32[]{:T(128)}, ...), condition=%wide.region_10.11_spmd.clone, body=%wide.region_6.10_spmd.clone.sunk | while | flops 214302016 | bytes 22319484 | solution.py:138
  196.6 2.7 fusion.109
  213.4 2.7 fusion.109
  230.2 2.7 fusion.109
  247.1 2.7 fusion.109
  262.0 23.2 %copy.24 = f32[4,320,2,4,4,64]{5,4,3,2,1,0:T(4,128)} copy(f32[4,320,2,4,4,64]{1,5,4,0,2,3:T(8,128)} %bitcast.175) | data formatting | bytes 20971520 | tf_op jit(solution)/shard_map/transpose | solution.py:140
  285.2 20.9 %reshape.306 = f32[20,64,2048]{2,1,0:T(8,128)} reshape(f32[4,320,2,4,4,64]{5,4,3,2,1,0:T(4,128)} %copy.24) | data formatting | bytes 20971520 | tf_op jit(solution)/shard_map/reshape | solution.py:140
  306.2 3.5 broadcast_in_dim.74
  309.7 22.1 %scatter_fusion = f32[12,64,2048]{2,1,0:T(8,128)} fusion(f32[12,64,2048]{2,1,0:T(8,128)} %broadcast_in_dim.74, s32[20]{0:T(128)S(1)} %fusion.68, f32[20,64,2048]{2,1,0:T(8,128)} %reshape.306), kind=kCustom, calls=%fused_computation.1 | custom fusion | flops 2621440 | bytes 31457360 | tf_op jit(solution)/shard_map/scatter-add | solution.py:142
  331.8 3.3 convert.18
  336.5 10.3 %collective-permute-start.2 = (bf16[4,64,2048]{2,1,0:T(8,128)(2,1)}, bf16[4,64,2048]{2,1,0:T(8,128)(2,1)S(1)}, u32[]{:S(2)}, u32[]{:S(2)}) collective-permute-start(bf16[4,64,2048]{2,1,0:T(8,128)(2,1)} %get-tuple-element.200), channel_id=1, source_target_pairs={{0,2},{2,4},{4,6},{6,8},{8,10},{10,12},{12,14},{14,16},{16,18},{18... | collective-permute-start | bytes 3145736 | tf_op jit(solution)/shard_map/ppermute | solution.py:33
  349.5 4.4 collective-permute-done.2
  354.9 4.6 collective-permute-done.3
  359.5 2.6 fusion.63
  362.1 4.6 convolution_convert_fusion.1
  366.8 89.6 %reduce-scatter.2.cloned.1.call-done = bf16[512,3072]{1,0:T(8,128)(2,1)} async-done(((bf16[1024,3072]{1,0:T(8,128)(2,1)}), bf16[512,3072]{1,0:T(8,128)(2,1)}) %reduce-scatter.2.cloned.1.call-update) | async-done | bytes 3145744 | tf_op jit(solution)/shard_map/reduce_scatter | solution.py:157
  456.5 4.7 multiply_reduce_fusion
  462.3 101.8 %all-reduce.2.cloned.1.call-done = bf16[512,3072]{1,0:T(8,128)(2,1)} async-done(((bf16[512,3072]{1,0:T(8,128)(2,1)}), bf16[512,3072]{1,0:T(8,128)(2,1)}) %all-reduce.2.cloned.1.call-update) | async-done | bytes 3145744 | tf_op jit(solution)/shard_map/psum | solution.py:165
  564.1 5.4 convert_element_type.117
  (140 shorter events, 95.3 us)
Async XLA Ops:
  7.2 0.8 copy-start.14
  7.2 0.8 copy-start.10
  7.2 0.8 copy-start.12
  7.2 2.8 copy-start.8
  7.2 85.5 %all-gather.2.cloned.1.call-start = ((), (), s32[]{:S(2)}) async-start(), calls=%async_computation.1 | async-start | bytes 9437184 | tf_op jit(solution)/shard_map/all_gather | solution.py:64
  7.9 448.5 %reduce-scatter.2.cloned.1.call-start = ((), (), s32[]{:S(2)}) async-start(), calls=%async_computation.2 | async-start | bytes 9437184 | tf_op jit(solution)/shard_map/reduce_scatter | solution.py:157
  10.4 87.0 %copy-start = (f32[256,1024]{1,0:T(8,128)}, f32[256,1024]{1,0:T(8,128)S(1)}, u32[]{:S(2)}) copy-start(f32[256,1024]{1,0:T(8,128)S(1)} %get-tuple-element.197) | copy-start | bytes 3145732
  97.3 1.1 copy-start.6
  97.3 5.6 copy-start.9
  97.4 5.7 copy-start.13
  97.4 6.3 %copy-start.11 = (f32[1,256]{1,0:T(1,128)S(1)}, f32[1,256]{1,0:T(1,128)}, u32[]{:S(2)}) copy-start(f32[1,256]{1,0:T(1,128)} %param.29) | copy-start | bytes 3076
  97.4 7.2 %copy-start.15 = (s32[1,4]{1,0:T(1,128)S(1)}, s32[1,4]{1,0:T(1,128)}, u32[]{:S(2)}) copy-start(s32[1,4]{1,0:T(1,128)} %param.26) | copy-start | bytes 52
  98.5 9.2 %copy-start.5 = (bf16[256,2048]{1,0:T(8,128)(2,1)}, bf16[256,2048]{1,0:T(8,128)(2,1)S(1)}, u32[]{:S(2)}) copy-start(bf16[256,2048]{1,0:T(8,128)(2,1)S(1)} %slice.82) | copy-start | bytes 3145732
  98.5 17.1 %collective-permute-start = (bf16[256,2048]{1,0:T(8,128)(2,1)S(1)}, bf16[256,2048]{1,0:T(8,128)(2,1)}, u32[]{:S(2)}, u32[]{:S(2)}) collective-permute-start(bf16[256,2048]{1,0:T(8,128)(2,1)S(1)} %slice.82), channel_id=1, source_target_pairs={{0,2},{2,4},{4,6},{6,8},{8,10},{10,12},{12,14},{14,16},{16,18},{18... | collective-permute-start | bytes 3145736 | tf_op jit(solution)/shard_map/ppermute | solution.py:21
  98.5 17.1 %collective-permute-start.1 = (bf16[256,2048]{1,0:T(8,128)(2,1)S(1)}, bf16[256,2048]{1,0:T(8,128)(2,1)}, u32[]{:S(2)}, u32[]{:S(2)}) collective-permute-start(bf16[256,2048]{1,0:T(8,128)(2,1)S(1)} %slice.82), channel_id=1, source_target_pairs={{2,0},{4,2},{6,4},{8,6},{10,8},{12,10},{14,12},{16,14},{18,16},{20... | collective-permute-start | bytes 3145736 | tf_op jit(solution)/shard_map/ppermute | solution.py:23
  140.4 17.9 %copy-start.3 = (bf16[4,4,64,4,64]{2,4,3,1,0:T(8,128)(2,1)S(1)}, bf16[4,4,64,4,64]{2,4,3,1,0:T(8,128)(2,1)}, u32[]{:S(2)}) copy-start(bf16[4,4,64,4,64]{2,4,3,1,0:T(8,128)(2,1)} %custom-call.2) | copy-start | bytes 1572868
  184.3 1.0 copy-start.4
  189.4 2.5 copy-start.1
  336.5 17.4 %collective-permute-start.2 = (bf16[4,64,2048]{2,1,0:T(8,128)(2,1)}, bf16[4,64,2048]{2,1,0:T(8,128)(2,1)S(1)}, u32[]{:S(2)}, u32[]{:S(2)}) collective-permute-start(bf16[4,64,2048]{2,1,0:T(8,128)(2,1)} %get-tuple-element.200), channel_id=1, source_target_pairs={{0,2},{2,4},{4,6},{6,8},{8,10},{10,12},{12,14},{14,16},{16,18},{18... | collective-permute-start | bytes 3145736 | tf_op jit(solution)/shard_map/ppermute | solution.py:33
  346.8 12.6 %collective-permute-start.3 = (bf16[4,64,2048]{2,1,0:T(8,128)(2,1)}, bf16[4,64,2048]{2,1,0:T(8,128)(2,1)}, u32[]{:S(2)}, u32[]{:S(2)}) collective-permute-start(bf16[4,64,2048]{2,1,0:T(8,128)(2,1)} %get-tuple-element.201), channel_id=1, source_target_pairs={{0,30},{2,0},{4,2},{6,4},{8,6},{10,8},{12,10},{14,12},{16,14},{18,... | collective-permute-start | bytes 3145736 | tf_op jit(solution)/shard_map/ppermute | solution.py:33
  349.5 12.6 %copy-start.2 = (f32[256,1024]{1,0:T(8,128)S(1)}, f32[256,1024]{1,0:T(8,128)}, u32[]{:S(2)}) copy-start(f32[256,1024]{1,0:T(8,128)} %copy-done) | copy-start | bytes 3145732
  353.9 1.0 copy-start.7
  366.8 197.4 %all-reduce.2.cloned.1.call-start = ((), (), s32[]{:S(2)}) async-start(), calls=%async_computation.3 | async-start | bytes 6291456 | tf_op jit(solution)/shard_map/psum | solution.py:165
Sparse Core Ops, SparseCore 0:
  9.6 83.0 all-gather.1
  366.9 89.5 reduce-scatter.1
  460.5 103.6 all-reduce.1
where the time goes:
time: 580 us; the launch traced here: 576 us
  waiting for transfers between devices  291 us (50%)
  local copies, waits for them, and re-layouts  130 us (22%)
  matrix products  68.9 us (12%)
  other arithmetic  56.3 us (10%)
  starting transfers between devices  14.9 us (3%)
  between operations  14 us (2%)
    psum x1, waiting for transfers between devices, body(): grad = lax.psum(partial_grad, 'seq').astype(jnp.float32)  102 us
    reduce_scatter x1, waiting for transfers between devices, body(): lax.psum_scatter(jnp.einsum('tc,tk->ck', columns, d_qkv, preferred_elemen...  89.6 us
    all_gather x1, waiting for transfers between devices, body(): lax.all_gather(w_qkv, 'fsdp', axis=0, tiled=True)  82.3 us
    transpose x1, local copies, waits for them, and re-layouts, body(): d_pair_groups.transpose(1, 2, 3, 0, 4, 5)  23.2 us
    scatter-add x1, other arithmetic, body(): jnp.zeros((ext_blocks, BLK, 2 * width), jnp.float32)  22.1 us
    unnamed x34, local copies, waits for them, and re-layouts  21.5 us
    reshape x1, local copies, waits for them, and re-layouts, body(): d_pair_groups.transpose(1, 2, 3, 0, 4, 5)  20.9 us
    reshape x1, local copies, waits for them, and re-layouts, body(): extended[ext_index]  18.6 us
  transfers between devices with their start and end apart: 7, of which 6 were waited for; matrix products, arithmetic and copies ran while one was open for 3% of the time, Pallas kernels for 0%

commit v1 on v0

--- a/solution.py
+++ b/solution.py
@@ -9,6 +9,11 @@
 REACH = 4
 NB = 5
 EPS = 1e-05
+
+
+def add_all(shard, axis):
+    parts = lax.all_gather(shard, axis)
+    return jnp.sum(parts, axis=0)
 
 
 def extended_2(cells, sides, width):
@@ -162,7 +167,7 @@
         scatter_dimension=0,
         tiled=True,
     )
-    grad = lax.psum(partial_grad, "seq").astype(jnp.float32)
+    grad = add_all(partial_grad, "seq").astype(jnp.float32)
     d_normed = lax.dot_general(
         d_qkv,
         lax.all_gather(w_qkv, "fsdp", axis=0, tiled=True),

time: 580 us -> 720 us (1.24)
  waiting for transfers between devices: 291 us -> 438 us
  other arithmetic: 56.3 us -> 64.1 us
    all_gather x0 -> x1, waiting for transfers between devices: none -> 243 us  [add_all(): parts = lax.all_gather(shard, axis)]
    psum x1 -> x0, waiting for transfers between devices: 102 us -> none  [body(): grad = lax.psum(partial_grad, 'seq').astype(jnp.float32)]
    reduce_sum x0 -> x1, other arithmetic: none -> 17 us  [add_all(): return jnp.sum(parts, axis=0)]
    ppermute x1, waiting for transfers between devices: 0.01 us -> 7.44 us  [extended_2(): lax.ppermute(head, axis, [((i + 1) % count, i) for i in range(count)])]
    unnamed x34 -> x30, local copies, waits for them, and re-layouts: 21.5 us -> 20.3 us
  transfers between devices with their start and end apart: 7 -> 7, of which waited for: 6 -> 7; matrix products, arithmetic and copies ran while one was open for 3% -> 2% of each run, Pallas kernels for 0% -> 0%
where the time goes in v1:
time: 720 us; the launch traced here: 717 us
  waiting for transfers between devices  438 us (61%)
  local copies, waits for them, and re-layouts  127 us (18%)
  matrix products  65.2 us (9%)
  other arithmetic  64.1 us (9%)
  between operations  14.1 us (2%)
  starting transfers between devices  8.73 us (1%)
    all_gather x1, waiting for transfers between devices, add_all(): parts = lax.all_gather(shard, axis)  243 us
    reduce_scatter x1, waiting for transfers between devices, body(): lax.psum_scatter(jnp.einsum('tc,tk->ck', columns, d_qkv, preferred_elemen...  89.4 us
    all_gather x1, waiting for transfers between devices, body(): lax.all_gather(w_qkv, 'fsdp', axis=0, tiled=True)  82.3 us
    transpose x1, local copies, waits for them, and re-layouts, body(): d_pair_groups.transpose(1, 2, 3, 0, 4, 5)  23.2 us
    scatter-add x1, other arithmetic, body(): jnp.zeros((ext_blocks, BLK, 2 * width), jnp.float32)  22.1 us
    reshape x1, local copies, waits for them, and re-layouts, body(): d_pair_groups.transpose(1, 2, 3, 0, 4, 5)  20.9 us
    unnamed x30, local copies, waits for them, and re-layouts  20.3 us
    reshape x1, local copies, waits for them, and re-layouts, body(): extended[ext_index]  18.6 us
  transfers between devices with their start and end apart: 7, of which 7 were waited for; matrix products, arithmetic and copies ran while one was open for 2% of the time, Pallas kernels for 0%

profile of v1, /device:TPU:0, one launch (start us, length us, event | category | flops | bytes accessed | tf_op | source)
XLA Modules:
  0.0 717.0 jit_solution(4535415521376863873)
XLA Ops:
  10.4 82.3 %all-gather.4.cloned.1.call-done = bf16[1024,3072]{1,0:T(8,128)(2,1)} async-done(((bf16[512,3072]{1,0:T(8,128)(2,1)}), bf16[1024,3072]{1,0:T(8,128)(2,1)}) %all-gather.4.cloned.1.call-update) | async-done | bytes 6291472 | tf_op jit(solution)/shard_map/all_gather | solution.py:69
  92.7 4.6 convolution_convert_fusion.2
  98.5 3.7 collective-permute-start.1
  107.0 7.4 %collective-permute-done.1 = bf16[256,2048]{1,0:T(8,128)(2,1)} collective-permute-done((bf16[256,2048]{1,0:T(8,128)(2,1)S(1)}, bf16[256,2048]{1,0:T(8,128)(2,1)}, u32[]{:S(2)}, u32[]{:S(2)}) %collective-permute-start.1) | collective-permute-done | bytes 1048608 | tf_op jit(solution)/shard_map/ppermute | solution.py:28
  114.5 4.8 collective-permute-done
  121.3 4.1 gather_fusion
  125.5 18.6 %reshape.286 = bf16[4,320,2,4,4,64]{5,4,3,2,1,0:T(4,128)(2,1)} reshape(bf16[20,64,2048]{2,1,0:T(8,128)(2,1)} %gather_fusion) | data formatting | bytes 10485760 | tf_op jit(solution)/shard_map/reshape | solution.py:82
  144.1 17.9 %copy.19 = bf16[4,4,320,2,4,64]{2,5,4,1,3,0:T(8,128)(2,1)} copy(bf16[4,4,320,2,4,64]{5,4,0,3,2,1:T(4,128)(2,1)} %bitcast.175) | data formatting | bytes 10485760
  162.0 26.0 %while.28 = (s32[]{:T(128)}, bf16[4,4,64,4,64]{2,4,3,1,0:T(8,128)(2,1)S(1)}, bf16[4,4,320,2,4,64]{2,5,4,1,3,0:T(8,128)(2,1)}, bf16[4,4,64,4,64]{4,2,3,1,0:T(8,128)(2,1)}, pred[4,5]{1,0:T(4,128)(4,1)S(1)}, /*index=5*/s32[]{:T(128)}) while((s32[]{:T(128)}, bf16[4,4,64,4,64]{2,4,3,1,0:T(8,128)(2,1)S(1)}, ...), condition=%wide.region_4.5_spmd.clone, body=%wide.region_1.4_spmd.clone.sunk | while | flops 128845440 | bytes 5787497 | solution.py:105
  165.4 3.0 fusion.100
  171.9 3.0 fusion.100
  178.4 3.0 fusion.100
  184.9 3.0 fusion.100
  191.1 2.9 reshape.293
  194.6 57.7 %while.29 = (s32[]{:T(128)}, bf16[4,4,64,4,64]{2,4,3,1,0:T(8,128)(2,1)}, f32[4,4,320,2,4,64]{2,5,4,1,3,0:T(8,128)}, bf16[4,4,320,2,4,64]{2,5,4,1,3,0:T(8,128)(2,...) while((s32[]{:T(128)}, ...), condition=%wide.region_10.11_spmd.clone, body=%wide.region_6.10_spmd.clone.sunk | while | flops 214302016 | bytes 35685928 | solution.py:143
  198.0 2.7 fusion.109
  212.4 2.7 fusion.109
  226.9 2.7 fusion.109
  241.4 2.7 fusion.109
  252.3 23.2 %copy.24 = f32[4,320,2,4,4,64]{5,4,3,2,1,0:T(4,128)} copy(f32[4,320,2,4,4,64]{1,5,4,0,2,3:T(8,128)} %bitcast.177) | data formatting | bytes 20971520 | tf_op jit(solution)/shard_map/transpose | solution.py:145
  275.5 20.9 %reshape.306 = f32[20,64,2048]{2,1,0:T(8,128)} reshape(f32[4,320,2,4,4,64]{5,4,3,2,1,0:T(4,128)} %copy.24) | data formatting | bytes 20971520 | tf_op jit(solution)/shard_map/reshape | solution.py:145
  296.5 3.5 broadcast_in_dim.74
  300.0 22.1 %scatter_fusion = f32[12,64,2048]{2,1,0:T(8,128)} fusion(f32[12,64,2048]{2,1,0:T(8,128)} %broadcast_in_dim.74, s32[20]{0:T(128)S(1)} %fusion.68, f32[20,64,2048]{2,1,0:T(8,128)} %reshape.306), kind=kCustom, calls=%fused_computation.1 | custom fusion | flops 2621440 | bytes 31457360 | tf_op jit(solution)/shard_map/scatter-add | solution.py:147
  322.1 3.3 convert.19
  326.8 4.9 collective-permute-start.2
  334.5 9.7 %collective-permute-done.2 = bf16[4,64,2048]{2,1,0:T(8,128)(2,1)} collective-permute-done((bf16[4,64,2048]{2,1,0:T(8,128)(2,1)}, bf16[4,64,2048]{2,1,0:T(8,128)(2,1)}, u32[]{:S(2)}, u32[]{:S(2)}) %collective-permute-start.2) | collective-permute-done | bytes 1048608 | tf_op jit(solution)/shard_map/ppermute | solution.py:38
  347.0 4.6 convolution_convert_fusion.1
  351.7 89.4 %reduce-scatter.2.cloned.1.call-done = bf16[512,3072]{1,0:T(8,128)(2,1)} async-done(((bf16[1024,3072]{1,0:T(8,128)(2,1)}), bf16[512,3072]{1,0:T(8,128)(2,1)}) %reduce-scatter.2.cloned.1.call-update) | async-done | bytes 3145744 | tf_op jit(solution)/shard_map/reduce_scatter | solution.py:162
  441.2 4.7 multiply_reduce_fusion
  447.0 242.9 %all-gather.6.cloned.1.call-done = bf16[8192,3072]{1,0:T(8,128)(2,1)} async-done(((bf16[512,3072]{1,0:T(8,128)(2,1)}), bf16[8192,3072]{1,0:T(8,128)(2,1)}) %all-gather.6.cloned.1.call-update) | async-done | bytes 50331664 | tf_op jit(solution)/shard_map/all_gather | solution.py:15
  690.0 17.0 %reduce_sum.72 = bf16[512,3072]{1,0:T(8,128)(2,1)S(1)} reduce(bf16[16,512,3072]{2,1,0:T(8,128)(2,1)} %bitcast.174, bf16[]{:T(256)} %constant.153.clone.1), dimensions={0}, to_apply=%region_14.15 | reduce | flops 23592960 | bytes 53477376 | tf_op jit(solution)/shard_map/reduce_sum | solution.py:16
  706.9 3.5 convert_element_type.119
  (178 shorter events, 83.3 us)
Async XLA Ops:
  7.2 2.8 copy-start.10
  7.2 85.5 %all-gather.4.cloned.1.call-start = ((), (), s32[]{:S(2)}) async-start(), calls=%async_computation.1 | async-start | bytes 9437184 | tf_op jit(solution)/shard_map/all_gather | solution.py:69
  7.9 433.2 %reduce-scatter.2.cloned.1.call-start = ((), (), s32[]{:S(2)}) async-start(), calls=%async_computation.2 | async-start | bytes 9437184 | tf_op jit(solution)/shard_map/reduce_scatter | solution.py:162
  10.4 87.0 %copy-start = (f32[256,1024]{1,0:T(8,128)}, f32[256,1024]{1,0:T(8,128)S(1)}, u32[]{:S(2)}) copy-start(f32[256,1024]{1,0:T(8,128)S(1)} %get-tuple-element.197) | copy-start | bytes 3145732
  97.3 4.8 copy-start.11
  97.4 5.5 copy-start.13
  97.4 6.4 copy-start.15
  97.4 6.6 copy-start.17
  98.5 8.5 %copy-start.6 = (bf16[256,2048]{1,0:T(8,128)(2,1)}, bf16[256,2048]{1,0:T(8,128)(2,1)S(1)}, u32[]{:S(2)}) copy-start(bf16[256,2048]{1,0:T(8,128)(2,1)S(1)} %slice.82) | copy-start | bytes 3145732
  98.5 16.0 %collective-permute-start.1 = (bf16[256,2048]{1,0:T(8,128)(2,1)S(1)}, bf16[256,2048]{1,0:T(8,128)(2,1)}, u32[]{:S(2)}, u32[]{:S(2)}) collective-permute-start(bf16[256,2048]{1,0:T(8,128)(2,1)S(1)} %slice.82), channel_id=1, source_target_pairs={{2,0},{4,2},{6,4},{8,6},{10,8},{12,10},{14,12},{16,14},{18,16},{20... | collective-permute-start | bytes 3145736 | tf_op jit(solution)/shard_map/ppermute | solution.py:28
  102.2 17.1 %collective-permute-start = (bf16[256,2048]{1,0:T(8,128)(2,1)S(1)}, bf16[256,2048]{1,0:T(8,128)(2,1)}, u32[]{:S(2)}, u32[]{:S(2)}) collective-permute-start(bf16[256,2048]{1,0:T(8,128)(2,1)S(1)} %slice.82), channel_id=1, source_target_pairs={{0,2},{2,4},{4,6},{6,8},{8,10},{10,12},{12,14},{14,16},{16,18},{18... | collective-permute-start | bytes 3145736 | tf_op jit(solution)/shard_map/ppermute | solution.py:26
  144.1 17.9 %copy-start.2 = (bf16[4,4,64,4,64]{2,4,3,1,0:T(8,128)(2,1)S(1)}, bf16[4,4,64,4,64]{2,4,3,1,0:T(8,128)(2,1)}, u32[]{:S(2)}) copy-start(bf16[4,4,64,4,64]{2,4,3,1,0:T(8,128)(2,1)} %custom-call.2) | copy-start | bytes 1572868
  191.1 2.9 copy-start.1
  194.6 1.8 copy-start.4
  200.7 2.0 copy-start.8
  204.1 1.6 copy-start.9
  207.1 1.9 copy-start.5
  209.0 1.7 copy-start.4
  215.1 2.0 copy-start.8
  218.5 1.6 copy-start.9
  221.5 2.0 copy-start.5
  223.5 1.7 copy-start.4
  229.6 2.0 copy-start.8
  233.0 1.6 copy-start.9
  236.0 2.0 copy-start.5
  238.0 1.7 copy-start.4
  244.1 2.0 copy-start.8
  247.5 1.6 copy-start.9
  250.5 1.9 copy-start.5
  326.8 17.3 %collective-permute-start.2 = (bf16[4,64,2048]{2,1,0:T(8,128)(2,1)}, bf16[4,64,2048]{2,1,0:T(8,128)(2,1)}, u32[]{:S(2)}, u32[]{:S(2)}) collective-permute-start(bf16[4,64,2048]{2,1,0:T(8,128)(2,1)} %get-tuple-element.200), channel_id=1, source_target_pairs={{0,2},{2,4},{4,6},{6,8},{8,10},{10,12},{12,14},{14,16},{16,18},{18... | collective-permute-start | bytes 3145736 | tf_op jit(solution)/shard_map/ppermute | solution.py:38
  331.8 12.6 %collective-permute-start.3 = (bf16[4,64,2048]{2,1,0:T(8,128)(2,1)}, bf16[4,64,2048]{2,1,0:T(8,128)(2,1)}, u32[]{:S(2)}, u32[]{:S(2)}) collective-permute-start(bf16[4,64,2048]{2,1,0:T(8,128)(2,1)} %get-tuple-element.201), channel_id=1, source_target_pairs={{0,30},{2,0},{4,2},{6,4},{8,6},{10,8},{12,10},{14,12},{16,14},{18,... | collective-permute-start | bytes 3145736 | tf_op jit(solution)/shard_map/ppermute | solution.py:38
  351.7 338.3 %all-gather.6.cloned.1.call-start = ((), (), s32[]{:S(2)}) async-start(), calls=%async_computation.3 | async-start | bytes 53477376 | tf_op jit(solution)/shard_map/all_gather | solution.py:15
  (9 other events, 10.3 us)
Sparse Core Ops, SparseCore 0:
  9.6 83.0 all-gather.3
  351.8 89.2 reduce-scatter.1
  442.8 247.0 all-gather.5
